TPU v7x, 256 devices: a whole 4x4x8 slice. The times are simulated.
256 devices in a mesh: tm: 32 (over y, x, core), space: 8 (over z).
Axes of the slice: x: 4, y: 4, z: 8, core: 2. Of those that a mesh axis runs over, the one named last changes fastest.
Arguments:
- latent_tokens: bfloat16 [64, 1792, 2240], P('tm', 'space'), may hold values from -6 to 6
- norm_gain: float32 [2240], replicated, may hold values from 0.5 to 1.5
- w_query: bfloat16 [2240, 1120], P('tm', 'space'), may hold values from -0.125 to 0.125
- w_key: bfloat16 [2240, 1120], P('tm', 'space'), may hold values from -0.125 to 0.125
- w_value: bfloat16 [2240, 1120], P('tm', 'space'), may hold values from -0.125 to 0.125
- out_gain: float32 [1120], replicated, may hold values from 0.5 to 1.5
- block_ids: int32 [64], P('tm'), may hold values from 0 to 15, never falling along the last dimension, each value on 1 to 8 neighbouring positions
Outputs:
- attended: bfloat16 [64, 1792, 1120], P('tm', 'space')
Inputs may be any that keep to these rules, and one draw needn't show every extreme that they name: `block_ids`: block numbers never fall from one frame to the next; each of the 16 blocks holds 1 to 8 frames and one holds exactly 8.
All inputs are finite; a program needn't handle non-finite values.
Results may differ from a plain program's by a relative error of at most 0.0065.
Values may be sent and summed in bfloat16 or wider, within the bound.
A program may use at most 192 MiB of HBM per device.

v0:
```python
import jax
import jax.numpy as jnp
from jax import lax
from jax.sharding import PartitionSpec as P

HEAD = 112
HEADS = 10


def prefix(value, axis, join, neutral):
    count, mine = (lax.axis_size(axis), lax.axis_index(axis))
    pieces = lax.all_gather(value, axis)
    so_far = jnp.full_like(value, 0) + jnp.asarray(neutral, value.dtype)

    def step(position, so_far):
        longer = join(so_far, pieces[position])
        return jnp.where(position < mine, longer, so_far)

    return lax.fori_loop(0, count - 1, step, so_far)


def carried_in(x, axis, join, neutral):
    count = lax.axis_size(axis)
    place = lax.axis_index(axis)
    ahead = count - 1 - place
    gathered = jax.tree.map(
        lambda a, kind: lax.all_gather(a.astype(kind), axis),
        x,
        jax.tree.map(lambda a: jnp.bfloat16 if a.dtype == jnp.float32 else a.dtype, x),
    )
    state = jax.tree.map(lambda a, e: jnp.zeros_like(a) + jnp.asarray(e, a.dtype), x, neutral)

    def one(step, state):
        source = count - 1 - step
        return join(
            state,
            jax.tree.map(
                lambda a, own: lax.dynamic_index_in_dim(a, source, 0, False).astype(own.dtype),
                gathered,
                x,
            ),
        )

    return lax.fori_loop(0, ahead, one, state)


def add_states(earlier, later):
    return earlier + later


def join_later(earlier, later):
    high_vacant, high_leading, high_uniform, high_running = earlier
    low_vacant, low_leading, low_uniform, low_running = later
    matching = (high_leading == low_leading).astype(jnp.float32)
    joined = low_uniform * matching * (1.0 - high_vacant)
    low_absent = low_vacant > 0.5
    leading = jnp.where(low_absent, high_leading, low_leading)
    vacant = low_vacant * high_vacant
    uniform = jnp.where(
        low_absent,
        high_uniform,
        low_uniform * (high_vacant + (1.0 - high_vacant) * high_uniform * matching),
    )
    running = jnp.where(low_absent, high_running, low_running + joined * high_running)
    return (vacant, leading, uniform, running)


def on_device(latent_tokens, norm_gain, w_query, w_key, w_value, out_gain, block_ids):
    frame_count, token_count, width = latent_tokens.shape
    row_count = frame_count * token_count
    values = latent_tokens.reshape(row_count, width).astype(jnp.float32)
    meansq = jnp.mean(values * values, axis=-1, keepdims=True)
    normed = (values * lax.rsqrt(meansq + 1e-06) * norm_gain).astype(jnp.bfloat16)
    stacked = jnp.stack((w_query, w_key, w_value))
    columns_full = lax.all_gather(stacked, "space", axis=2, tiled=True)
    projected = jnp.einsum(
        "rn,cnh->crh",
        normed,
        lax.all_gather(columns_full, "tm", axis=1, tiled=True),
        preferred_element_type=jnp.float32,
    )
    channels = projected.shape[2]
    query = jax.nn.relu(projected[0]).reshape(frame_count, token_count, HEADS, HEAD)
    key = (
        jax.nn.relu(projected[1])
        .astype(jnp.bfloat16)
        .reshape(frame_count, token_count, HEADS, HEAD)
    )
    value = projected[2].astype(jnp.bfloat16).reshape(frame_count, token_count, HEADS, HEAD)
    local_states = jnp.einsum("fthk,fthv->fhkv", key, value, preferred_element_type=jnp.float32)
    per_frame_state = lax.psum(local_states, "space")
    device_sum = jnp.sum(per_frame_state, axis=0)
    zero_state = jnp.zeros_like(device_sum)
    before = prefix(device_sum, "tm", add_states, zero_state)
    leading_id = block_ids[0]
    closing_id = block_ids[frame_count - 1]
    within_leading = (block_ids == leading_id).astype(jnp.float32)
    leading_sum = jnp.einsum(
        "o,owpe->wpe", within_leading, per_frame_state, precision=lax.Precision.HIGHEST
    )
    uniform_flag = jnp.min(within_leading)
    leading_float = leading_id.astype(jnp.float32)
    closing_float = closing_id.astype(jnp.float32)
    summary = (jnp.float32(0.0), leading_float, uniform_flag, leading_sum)
    identity = (jnp.float32(1.0), jnp.float32(0.0), jnp.float32(1.0), zero_state)
    vacant, leading, uniform, running = carried_in(summary, "tm", join_later, identity)
    reaches = (1.0 - vacant) * (leading == closing_float).astype(jnp.float32)
    trailing = reaches * running
    earlier_mask = (block_ids[None, :] <= block_ids[:, None]).astype(jnp.float32)
    in_closing = (block_ids == closing_id).astype(jnp.float32)
    carried = before[None] + jnp.einsum(
        "ij,jhkv->ihkv", earlier_mask, per_frame_state, precision=lax.Precision.HIGHEST
    )
    carried = carried + in_closing[:, None, None, None] * trailing[None]
    numerator = jnp.einsum("fthk,fhkv->fthv", query, carried, precision=lax.Precision.HIGHEST)
    head_meansq = jnp.mean(numerator * numerator, axis=-1, keepdims=True)
    result = numerator * lax.rsqrt(head_meansq + 1e-06) * out_gain.reshape(HEADS, HEAD)
    return result.reshape(frame_count, token_count, channels).astype(jnp.bfloat16)


def solution(mesh):
    placed = (
        P("tm", "space", None),
        P(),
        P("tm", "space"),
        P("tm", "space"),
        P("tm", "space"),
        P(),
        P("tm"),
    )
    return jax.shard_map(
        on_device, mesh=mesh, in_specs=placed, out_specs=P("tm", "space", None), check_vma=False
    )
```

profile of v0, /device:TPU:32, one launch (start us, length us, event | category | flops | bytes accessed | tf_op | source)
XLA Modules:
  0.0 544.3 jit_solution(14924308415363143273)
XLA Ops:
  7.7 29.9 %all_gather.33 = bf16[3,70,1120]{1,0,2:T(4,128)(2,1)S(1)} all-gather(bf16[3,70,140]{1,0,2:T(4,128)(2,1)S(1)} %copy.37), channel_id=1, replica_groups=mesh['tm'=32,'space'=8] {'space'}, dimensions={2}, use_global_device_ids=true | all-gather | bytes 529200 | tf_op jit(solution)/shard_map/all_gather | solution.py:75
  37.6 2.2 copy.38
  40.5 1.9 fusion.7
  42.4 84.1 %all-gather.6.cloned.1.call-done = bf16[3,2240,1120]{2,0,1:T(4,128)(2,1)} async-done(((bf16[3,70,1120]{2,0,1:T(4,128)(2,1)}), bf16[3,2240,1120]{2,0,1:T(4,128)(2,1)}) %all-gather.6.cloned.1.call-update) | async-done | bytes 15052816 | tf_op jit(solution)/shard_map/all_gather | solution.py:79
  126.5 14.1 %fusion.3 = f32[3,448,1120]{2,1,0:T(8,128)S(1)} fusion(bf16[3,2240,1120]{2,0,1:T(4,128)(2,1)} %all-gather.6.cloned.1.call-done, bf16[448,2240]{1,0:T(8,128)(2,1)} %fusion.7), kind=kOutput, calls=%fused_computation.5 | convolution fusion | flops 6743654400 | bytes 23080960 | tf_op jit(solution)/shard_map/rn,cnh->crh/dot_general | solution.py:76
  140.7 1.4 fusion.13
  142.1 1.5 copy-done.2
  143.6 3.4 reshape.84
  147.0 3.1 reshape.83
  150.1 3.1 fusion.16
  153.9 75.4 %all-reduce.6.cloned.1.call-done = f32[2,10,112,112]{3,2,1,0:T(8,128)} async-done(((f32[2,10,112,112]{3,2,1,0:T(8,128)}), f32[2,10,112,112]{3,2,1,0:T(8,128)}) %all-reduce.6.cloned.1.call-update) | async-done | bytes 1003536 | tf_op jit(solution)/shard_map/psum | solution.py:91
  229.3 4.7 fusion.20
  239.7 1.3 dynamic-update-slice.2
  241.0 63.4 %all-reduce.3 = (bf16[32]{0:T(256)(128)(2,1)S(1)}, bf16[32]{0:T(256)(128)(2,1)S(1)}, bf16[32]{0:T(256)(128)(2,1)S(1)}) all-reduce(bf16[32]{0:T(256)(128)(2,1)S(1)} %dynamic-update-slice, bf16[32]{0:T(256)(128)(2,1)S(1)} %dynamic-update-slice.1, bf16[32]{0:T(256)(128)(2,1)S(1)} %dynamic-update-slice.2), channel_id=1, replica_groups=mesh['tm'=32,'space'=8] {'tm'}, use_global_device_ids=true, to_apply=%add | all-reduce | flops 96 | bytes 384
  305.6 1.7 slice_maximum_fusion
  307.4 3.3 reshape.85
  310.7 177.9 %while.32 = (s32[]{:T(128)}, f32[]{:T(128)}, f32[]{:T(128)}, f32[10,112,112]{2,1,0:T(8,128)S(1)}, s32[]{:T(128)}, /*index=5*/bf16[32]{0:T(256)(128)(2,1)S(1)}, b...) while((s32[]{:T(128)}, f32[]{:T(128)}, f32[]{:T(128)}, ...), condition=%wide.region_7.8_spmd, body=%wide.region_6.7_spmd.sunk | while | flops 501773 | bytes 1254722 | solution.py:44
  320.9 1.3 fusion.33
  361.1 1.3 fusion.33
  488.6 38.9 %while.33 = (s32[]{:T(128)}, f32[10,112,112]{2,1,0:T(8,128)S(1)}, s32[]{:T(128)}, f32[32,10,112,112]{3,2,1,0:T(8,128)}, s32[]{:T(128)}, /*index=5*/s32[]{:T(128)}) while((s32[]{:T(128)}, f32[10,112,112]{2,1,0:T(8,128)S(1)}, s32[]{:T(128)}, f32[32,10,112,112]{3,2,1,0:T(8,128)}, s32[]{:T(128)}, /*index=5*/s32[]{:T(128)}) %tuple.73), condition=%wide.region_4.5_spmd.clone, body=%wide.region_3.4_spmd.clone.sunk | while | flops 376324 | bytes 1505381 | solution.py:19
  488.6 1.3 add_select_fusion.2
  527.6 3.3 fusion.15
  530.9 5.1 fusion.8
  536.4 1.4 copy.48
  (201 shorter events, 133.8 us)
Async XLA Ops:
  6.5 120.0 %all-gather.6.cloned.1.call-start = ((), (), s32[]{:S(2)}) async-start(), calls=%async_computation | async-start | bytes 21288960 | tf_op jit(solution)/shard_map/all_gather | solution.py:79
  6.5 33.4 %copy-start.1 = (bf16[2,224,2240]{2,1,0:T(8,128)(2,1)S(1)}, bf16[2,224,2240]{2,1,0:T(8,128)(2,1)}, u32[]{:S(2)}) copy-start(bf16[2,224,2240]{2,1,0:T(8,128)(2,1)} %param.11) | copy-start | bytes 6021124
  37.6 2.9 copy-start.5
  39.9 189.4 %all-reduce.6.cloned.1.call-start = ((), (), s32[]{:S(2)}) async-start(), calls=%async_computation.1 | async-start | bytes 2293760 | tf_op jit(solution)/shard_map/psum | solution.py:91
  140.7 2.9 copy-start.2
  150.1 3.2 copy-start.7
  153.3 157.4 %all-gather.10.cloned.1.call-start = ((), (), s32[]{:S(2)}) async-start(), calls=%async_computation.3 | async-start | bytes 9461760 | tf_op jit(solution)/shard_map/all_gather | solution.py:27
  229.3 5.6 %copy-start.3 = (f32[2,10,112,112]{3,2,1,0:T(8,128)S(1)}, f32[2,10,112,112]{3,2,1,0:T(8,128)}, u32[]{:S(2)}) copy-start(f32[2,10,112,112]{3,2,1,0:T(8,128)} %all-reduce.6.cloned.1.call-done) | copy-start | bytes 3010564
  234.0 2.5 copy-start.8
  234.0 71.0 %copy-start.6 = (f32[1120]{0:T(1024)S(1)}, f32[1120]{0:T(1024)}, u32[]{:S(2)}) copy-start(f32[1120]{0:T(1024)} %param.16) | copy-start | bytes 13444
  234.8 253.8 %all-gather.8.cloned.1.call-start = ((), (), s32[]{:S(2)}) async-start(), calls=%async_computation.2 | async-start | bytes 18923520 | tf_op jit(solution)/shard_map/all_gather | solution.py:12
  488.6 38.9 %copy-start.4 = (f32[2,10,112,112]{3,2,1,0:T(8,128)S(1)}, f32[2,10,112,112]{3,2,1,0:T(8,128)}, u32[]{:S(2)}) copy-start(f32[2,10,112,112]{3,2,1,0:T(8,128)} %all-reduce.6.cloned.1.call-done) | copy-start | bytes 3010564
  527.6 3.3 copy-start
Sparse Core Ops, SparseCore 0:
  40.0 86.5 all-gather.5
  153.4 75.8 all-reduce.5
  235.0 58.7 all-gather.9
  296.1 80.6 all-gather.7
where the time goes:
time: 548 us; the launch traced here: 544 us
  waiting for transfers between devices  160 us (29%)
  blocking collectives  93.3 us (17%)
  loops' own time  87.7 us (16%)
  other arithmetic  87.5 us (16%)
  local copies, waits for them, and re-layouts  71.2 us (13%)
  matrix products  30.4 us (6%)
  between operations  14.5 us (3%)
    another operation x1, loops' own time, carried_in(): return lax.fori_loop(0, ahead, one, state)  86.9 us
    all_gather x1, waiting for transfers between devices, on_device(): lax.all_gather(columns_full, 'tm', axis=1, tiled=True)  84.1 us
    psum x1, waiting for transfers between devices, on_device(): per_frame_state = lax.psum(local_states, 'space')  75.4 us
    unnamed x1, blocking collectives  63.4 us
    dynamic_slice x93, local copies, waits for them, and re-layouts, one(): lax.dynamic_index_in_dim(a, source, 0, False).astype(own.dtype)  52 us
    select_n x31, other arithmetic, join_later(): jnp.where(low_absent, high_running, low_running + joined * high_running)  38.9 us
    select_n x31, other arithmetic, step(): return jnp.where(position < mine, longer, so_far)  38.2 us
    all_gather x1, blocking collectives, on_device(): columns_full = lax.all_gather(stacked, 'space', axis=2, tiled=True)  29.9 us
  transfers between devices with their start and end apart: 4, of which 2 were waited for; matrix products, arithmetic and copies ran while one was open for 19% of the time, Pallas kernels for 0%

commit v1 on v0

v1 whole, which is shorter than its diff:
```python
import jax
import jax.numpy as jnp
from jax import lax
from jax.sharding import PartitionSpec as P

HEAD = 112
HEADS = 10


def gathered(weights):
    columns_full = lax.all_gather(jnp.stack(weights), "space", axis=2, tiled=True)
    return lax.all_gather(columns_full, "tm", axis=1, tiled=True)


def on_device(latent_tokens, norm_gain, w_query, w_key, w_value, out_gain, block_ids):
    frame_count, token_count, width = latent_tokens.shape
    row_count = frame_count * token_count
    values = latent_tokens.reshape(row_count, width).astype(jnp.float32)
    meansq = jnp.mean(values * values, axis=-1, keepdims=True)
    normed = (values * lax.rsqrt(meansq + 1e-06) * norm_gain).astype(jnp.bfloat16)
    pair = gathered((w_key, w_value))
    alone = gathered((w_query,))
    projected = jnp.einsum("rn,cnh->crh", normed, pair, preferred_element_type=jnp.float32)
    channels = projected.shape[2]
    headed = (frame_count, token_count, HEADS, HEAD)
    key = jax.nn.relu(projected[0]).astype(jnp.bfloat16).reshape(headed)
    value = projected[1].astype(jnp.bfloat16).reshape(headed)
    states = jnp.einsum("fthk,fthv->fhkv", key, value, preferred_element_type=jnp.float32)
    states = states.reshape(frame_count, channels, HEAD)
    mine = lax.psum_scatter(states, "space", scatter_dimension=1, tiled=True)
    everyone = lax.all_gather(mine.astype(jnp.bfloat16), "tm", tiled=True)
    all_ids = lax.all_gather(block_ids, "tm", tiled=True)
    reaches = (all_ids[None, :] <= block_ids[:, None]).astype(jnp.bfloat16)
    carried = jnp.einsum("fg,gkv->fkv", reaches, everyone, preferred_element_type=jnp.float32)
    carried = lax.all_gather(carried.astype(jnp.bfloat16), "space", axis=1, tiled=True)
    carried = carried.reshape(frame_count, HEADS, HEAD, HEAD)
    query = jnp.einsum("rn,cnh->crh", normed, alone, preferred_element_type=jnp.float32)[0]
    query = jax.nn.relu(query).astype(jnp.bfloat16).reshape(headed)
    numerator = jnp.einsum("fthk,fhkv->fthv", query, carried, preferred_element_type=jnp.float32)
    head_meansq = jnp.mean(numerator * numerator, axis=-1, keepdims=True)
    result = numerator * lax.rsqrt(head_meansq + 1e-06) * out_gain.reshape(HEADS, HEAD)
    return result.reshape(frame_count, token_count, channels).astype(jnp.bfloat16)


def solution(mesh):
    placed = (
        P("tm", "space", None),
        P(),
        P("tm", "space"),
        P("tm", "space"),
        P("tm", "space"),
        P(),
        P("tm"),
    )
    return jax.shard_map(
        on_device, mesh=mesh, in_specs=placed, out_specs=P("tm", "space", None), check_vma=False
    )
```

time: 548 us -> 275 us (0.50)
  waiting for transfers between devices: 160 us -> 46.7 us
  loops' own time: 87.7 us -> 0 us
  other arithmetic: 87.5 us -> 6.73 us
  blocking collectives: 93.3 us -> 155 us
  local copies, waits for them, and re-layouts: 71.2 us -> 29.9 us
  matrix products: 30.4 us -> 20.5 us
    another operation x2 -> x0, loops' own time: 87.7 us -> none  [the longest x1 86.9 us: carried_in(): return lax.fori_loop(0, ahead, one, state)]
    select_n x62 -> x0, other arithmetic: 77.1 us -> none  [the longest x31 38.9 us: join_later(): jnp.where(low_absent, high_running, low_running + joined * high_running)]
    psum x1 -> x0, waiting for transfers between devices: 75.4 us -> none  [on_device(): per_frame_state = lax.psum(local_states, 'space')]
    dynamic_slice x93 -> x0, local copies, waits for them, and re-layouts: 52 us -> none  [one(): lax.dynamic_index_in_dim(a, source, 0, False).astype(own.dtype)]
    all_gather x1 -> x3, blocking collectives: 29.9 us -> 79 us  [the longest x2 53.1 us: gathered(): lax.all_gather(jnp.stack(weights), 'space', axis=2, tiled=True)]
    all_gather x3, waiting for transfers between devices: 84.2 us -> 46.7 us  [the longest x2 32.9 us: gathered(): return lax.all_gather(columns_full, 'tm', axis=1, tiled=True)]
    unnamed x1 -> x2, blocking collectives: 63.4 us -> 76.1 us
    dot_general x4, matrix products: 27.2 us -> 17.9 us  [the longest x1 9.52 us: on_device(): jnp.einsum('rn,cnh->crh', normed, pair, preferred_element_type=jnp.float32)]
  transfers between devices with their start and end apart: 4 -> 3, of which waited for: 2 -> 2; matrix products, arithmetic and copies ran while one was open for 19% -> 18% of each run, Pallas kernels for 0% -> 0%
where the time goes in v1:
time: 275 us; the launch traced here: 274 us
  blocking collectives  155 us (56%)
  waiting for transfers between devices  46.7 us (17%)
  local copies, waits for them, and re-layouts  29.9 us (11%)
  matrix products  20.5 us (7%)
  between operations  14.4 us (5%)
  other arithmetic  6.73 us (2%)
    unnamed x2, blocking collectives  76.1 us
    all_gather x2, blocking collectives, gathered(): lax.all_gather(jnp.stack(weights), 'space', axis=2, tiled=True)  53.1 us
    all_gather x2, waiting for transfers between devices, gathered(): return lax.all_gather(columns_full, 'tm', axis=1, tiled=True)  32.9 us
    all_gather x1, blocking collectives, on_device(): lax.all_gather(carried.astype(jnp.bfloat16), 'space', axis=1, tiled=True)  26 us
    all_gather x1, waiting for transfers between devices, on_device(): everyone = lax.all_gather(mine.astype(jnp.bfloat16), 'tm', tiled=True)  13.7 us
    unnamed x24, local copies, waits for them, and re-layouts  10.6 us
    dot_general x1, matrix products, on_device(): jnp.einsum('rn,cnh->crh', normed, pair, preferred_element_type=jnp.float32)  9.52 us
  transfers between devices with their start and end apart: 3, of which 2 were waited for; matrix products, arithmetic and copies ran while one was open for 18% of the time, Pallas kernels for 0%

profile of v1, /device:TPU:32, one launch (start us, length us, event | category | flops | bytes accessed | tf_op | source)
XLA Modules:
  0.0 273.5 jit_solution(4759564278663120340)
XLA Ops:
  6.5 0.9 pad_maximum_fusion
  7.6 28.2 %all_gather.22 = bf16[2,70,1120]{1,0,2:T(2,128)(2,1)S(1)} all-gather(bf16[2,70,140]{1,0,2:T(2,128)(2,1)S(1)} %copy.40), channel_id=1, replica_groups=mesh['tm'=32,'space'=8] {'space'}, dimensions={2}, use_global_device_ids=true | all-gather | bytes 352800 | tf_op jit(solution)/shard_map/all_gather | solution.py:11
  35.9 2.2 copy.41
  38.2 24.8 %all-gather.2 = bf16[8,140,70]{2,1,0:T(8,128)(2,1)S(1)} all-gather(bf16[1,140,70]{2,1,0:T(8,128)(2,1)S(1)} %bitcast.50), channel_id=2, replica_groups=mesh['tm'=32,'space'=8] {'space'}, dimensions={0}, use_global_device_ids=true | all-gather | bytes 176400 | tf_op jit(solution)/shard_map/all_gather | solution.py:11
  65.8 1.8 fusion.3
  67.7 32.9 %all-gather.8.cloned.1.call-done = bf16[2,2240,1120]{2,0,1:T(2,128)(2,1)} async-done(((bf16[2,70,1120]{2,0,1:T(2,128)(2,1)}), bf16[2,2240,1120]{2,0,1:T(2,128)(2,1)}) %all-gather.8.cloned.1.call-update) | async-done | bytes 10035216 | tf_op jit(solution)/shard_map/all_gather | solution.py:12
  100.6 9.5 %fusion.4 = bf16[2,448,1120]{2,1,0:T(8,128)(2,1)S(1)} fusion(bf16[2,2240,1120]{2,0,1:T(2,128)(2,1)} %all-gather.8.cloned.1.call-done, bf16[448,2240]{1,0:T(8,128)(2,1)} %fusion.3), kind=kOutput, calls=%fused_computation.7 | convolution fusion | flops 4495769600 | bytes 14049280 | tf_op jit(solution)/shard_map/rn,cnh->crh/dot_general | solution.py:23
  110.1 1.2 fusion.14
  111.3 4.4 %reshape.88 = bf16[2,224,10,112]{3,2,1,0:T(8,128)(2,1)} reshape(bf16[1,448,1120]{2,1,0:T(8,128)(2,1)} %get-tuple-element.5) | data formatting | bytes 2007040 | tf_op jit(solution)/shard_map/convert_element_type | solution.py:26
  115.7 3.1 %reshape.89 = bf16[2,224,10,112]{3,2,1,0:T(8,128)(2,1)} reshape(bf16[1,448,1120]{2,1,0:T(8,128)(2,1)S(1)} %get-tuple-element.6) | data formatting | bytes 2007040 | tf_op jit(solution)/shard_map/convert_element_type | solution.py:27
  118.8 2.6 fusion.18
  121.5 4.2 %copy.47 = f32[2,1120,112]{2,0,1:T(2,128)S(1)} copy(f32[2,1120,112]{2,1,0:T(8,128)S(1)} %bitcast.46) | data formatting | bytes 2007040 | tf_op jit(solution)/shard_map/reshape | solution.py:29
  125.7 61.3 %all-reduce.3 = bf16[2,1120,112]{2,0,1:T(2,128)(2,1)} all-reduce(f32[2,1120,112]{2,0,1:T(2,128)S(1)} %copy.47), channel_id=4, replica_groups=mesh['tm'=32,'space'=8] {'space'}, use_global_device_ids=true, to_apply=%region_1.2.clone | all-reduce | flops 250880 | bytes 1505280
  187.1 0.9 dynamic-slice_convert_fusion
  190.2 14.8 %all-reduce = s32[64]{0:T(128)S(1)} all-reduce(s32[64]{0:T(128)S(1)} %dynamic-update-slice), channel_id=1, replica_groups=mesh['tm'=32,'space'=8] {'tm'}, use_global_device_ids=true, to_apply=%add | all-reduce | flops 64 | bytes 512
  204.9 1.9 multiply_convert_fusion
  206.9 8.1 %reshape.83 = bf16[2240,1120]{1,0:T(8,128)(2,1)} reshape(bf16[32,70,1120]{2,1,0:T(8,128)(2,1)} %all-gather.12.cloned.1.call-done) | data formatting | bytes 10035200
  215.0 5.3 %fusion.8 = bf16[1,448,1120]{2,1,0:T(8,128)(2,1)S(1)} fusion(bf16[448,2240]{1,0:T(8,128)(2,1)S(1)} %bitcast.48, bf16[2240,1120]{1,0:T(8,128)(2,1)} %reshape.83), kind=kOutput, calls=%fused_computation.10 | convolution fusion | flops 2248888320 | bytes 8028160 | tf_op jit(solution)/shard_map/rn,cnh->crh/dot_general | solution.py:37
  220.3 2.2 reshape.91
  222.5 13.7 %all-gather.10.cloned.1.call-done = bf16[64,140,112]{2,1,0:T(8,128)(2,1)} async-done(((bf16[2,140,112]{2,1,0:T(8,128)(2,1)}), bf16[64,140,112]{2,1,0:T(8,128)(2,1)}) %all-gather.10.cloned.1.call-update) | async-done | bytes 2007056 | tf_op jit(solution)/shard_map/all_gather | solution.py:31
  236.2 2.2 fusion.21
  238.4 26.0 %all_gather.25 = bf16[2,1120,112]{2,0,1:T(2,128)(2,1)S(1)} all-gather(bf16[2,140,112]{2,0,1:T(2,128)(2,1)S(1)} %fusion.21), channel_id=1, replica_groups=mesh['tm'=32,'space'=8] {'space'}, dimensions={1}, use_global_device_ids=true | all-gather | bytes 564480 | tf_op jit(solution)/shard_map/all_gather | solution.py:35
  264.3 0.9 fusion.9
  265.6 1.4 copy.56
  (38 shorter events, 4.4 us)
Async XLA Ops:
  6.5 31.6 %copy-start.3 = (bf16[70,140]{1,0:T(8,128)(2,1)S(1)}, bf16[70,140]{1,0:T(8,128)(2,1)}, u32[]{:S(2)}) copy-start(bf16[70,140]{1,0:T(8,128)(2,1)} %param.9) | copy-start | bytes 58804
  6.5 57.6 %copy-start = (bf16[2,224,2240]{2,1,0:T(8,128)(2,1)S(1)}, bf16[2,224,2240]{2,1,0:T(8,128)(2,1)}, u32[]{:S(2)}) copy-start(bf16[2,224,2240]{2,1,0:T(8,128)(2,1)} %param.7) | copy-start | bytes 6021124
  6.5 94.1 %all-gather.8.cloned.1.call-start = ((), (), s32[]{:S(2)}) async-start(), calls=%async_computation | async-start | bytes 10644480 | tf_op jit(solution)/shard_map/all_gather | solution.py:12
  38.0 26.7 %copy-start.7 = (u32[256]{0:T(256)S(1)}, u32[256]{0:T(256)}, u32[]{:S(2)}) copy-start(u32[256]{0:T(256)} %constant.27) | copy-start | bytes 3076
  38.0 27.8 %copy-start.2 = (f32[2240]{0:T(1024)S(1)}, f32[2240]{0:T(1024)}, u32[]{:S(2)}) copy-start(f32[2240]{0:T(1024)} %param.8) | copy-start | bytes 26884
  38.0 168.8 %all-gather.12.cloned.1.call-start = ((), (), s32[]{:S(2)}) async-start(), calls=%async_computation.2 | async-start | bytes 5474304 | tf_op jit(solution)/shard_map/all_gather | solution.py:12
  64.0 172.2 %all-gather.10.cloned.1.call-start = ((), (), s32[]{:S(2)}) async-start(), calls=%async_computation.1 | async-start | bytes 2433024 | tf_op jit(solution)/shard_map/all_gather | solution.py:31
  121.5 67.2 %copy-start.4 = (f32[1120]{0:T(1024)S(1)}, f32[1120]{0:T(1024)}, u32[]{:S(2)}) copy-start(f32[1120]{0:T(1024)} %param.12) | copy-start | bytes 13444
  121.5 67.3 %copy-start.6 = (u32[256]{0:T(256)S(1)}, u32[256]{0:T(256)}, u32[]{:S(2)}) copy-start(u32[256]{0:T(256)} %constant.21) | copy-start | bytes 3076
  121.5 68.4 %copy-start.5 = (s32[2]{0:T(128)S(1)}, s32[2]{0:T(128)}, u32[]{:S(2)}) copy-start(s32[2]{0:T(128)} %param.13) | copy-start | bytes 28
  206.9 8.2 %copy-start.1 = (bf16[2,224,2240]{2,1,0:T(8,128)(2,1)S(1)}, bf16[2,224,2240]{2,1,0:T(8,128)(2,1)}, u32[]{:S(2)}) copy-start(bf16[2,224,2240]{2,1,0:T(8,128)(2,1)} %multiply_convert_fusion) | copy-start | bytes 6021124
Sparse Core Ops, SparseCore 0:
  38.2 62.4 all-gather.7
  103.2 52.1 all-gather.11
  188.8 47.4 all-gather.9
